TPU v7x, 128 devices: a whole 4x4x4 slice. The times are simulated.
128 devices in a mesh: req: 32 (over y, z, core), grp: 4 (over x).
Axes of the slice: x: 4, y: 4, z: 4, core: 2. Of those that a mesh axis runs over, the one named last changes fastest.
Arguments:
- hidden_in: bfloat16 [16384, 2048], P('req'), may hold values from -6 to 6
- attn_gain: float32 [2048], replicated, may hold values from 0.1 to 1.9
- mlp_gain: float32 [2048], replicated, may hold values from 0.1 to 1.9
- w_query: bfloat16 [2048, 2048], P(None, 'grp'), may hold values from -0.75 to 0.75
- w_key: bfloat16 [2048, 512], P(None, 'grp'), may hold values from -0.125 to 0.125
- w_value: bfloat16 [2048, 512], P(None, 'grp'), may hold values from -0.125 to 0.125
- w_out: bfloat16 [2048, 2048], P('grp'), may hold values from -0.125 to 0.125
- w_gate: bfloat16 [2048, 8192], P(None, 'req'), may hold values from -0.125 to 0.125
- w_up: bfloat16 [2048, 8192], P(None, 'req'), may hold values from -0.125 to 0.125
- w_down: bfloat16 [8192, 2048], P('req'), may hold values from -0.0625 to 0.0625
- cache_k: bfloat16 [16384, 16, 512], P('req', None, 'grp'), may hold values from -4000 to 4000
- cache_v: bfloat16 [16384, 16, 512], P('req', None, 'grp'), may hold values from -6 to 6
- owner_of_row: int32 [16384], P('req'), may hold values from 0 to 31, as said below
- new_len: int32 [32, 32], P('req'), may hold values from 0 to 32, as said below
- prior_len: int32 [32, 32], P('req'), may hold values from 0 to 256, as said below
- page_table: int32 [32, 512], P('req'), may hold values from 0 to 511, each once within a row
Outputs:
- layer_out: bfloat16 [16384, 2048], P(('req', 'grp'))
- new_cache_k: bfloat16 [16384, 16, 512], P('req', None, 'grp')
- new_cache_v: bfloat16 [16384, 16, 512], P('req', None, 'grp')
Inputs may be any that keep to these rules, and one draw needn't show every extreme that they name: `owner_of_row`: rows of one block of 512 that name the same owner are consecutive; each block holds at most one request for each owner, of at most 32 rows; in every draw one owner receives a request of exactly 32 rows from every block. new_len[o, s] is the number of rows of block s of owner_of_row that name o. prior_len[o, s] + new_len[o, s] <= 256.
All inputs are finite; a program needn't handle non-finite values.
Results may differ from a plain program's by a relative error of at most 0.0063.
Values may be sent and summed in bfloat16 or wider, within the bound.
A program may use at most 128 MiB of HBM per device.

v0:
```python
import jax
import jax.numpy as jnp
from jax import lax
from jax.sharding import PartitionSpec as P

HD = 64
PAGE = 16
MAXP = 16
CONTEXT = 256
EPSILON = 1e-05
RESIDUAL_MULT = 0.22
SCORE_MULT = 0.015625
ROPE_BASE = 10000000.0


def normalize(values, gain):
    mean_square = jnp.mean(values * values, axis=-1, keepdims=True)
    return values * lax.rsqrt(mean_square + EPSILON) * gain


def rotary(values, positions):
    dim = values.shape[-1]
    half = dim // 2
    freq = jnp.power(ROPE_BASE, -2.0 * jnp.arange(half, dtype=jnp.int32).astype(jnp.float32) / dim)
    angle = positions.astype(jnp.float32)[:, :, None] * freq
    cosine = jnp.cos(angle)[:, :, None, :]
    sine = jnp.sin(angle)[:, :, None, :]
    first = values[..., :half].astype(jnp.float32)
    second = values[..., half:].astype(jnp.float32)
    return jnp.concatenate(
        [first * cosine - second * sine, second * cosine + first * sine], axis=-1
    )


def source_layout(owner_block, peers, pair_rows):
    row_count = owner_block.shape[0]
    owners = jnp.arange(peers, dtype=jnp.int32)
    member = owner_block[None, :] == owners[:, None]
    counts = jnp.sum(member.astype(jnp.int32), axis=1)
    row_ids = jnp.arange(row_count, dtype=jnp.int32)
    starts = jnp.min(jnp.where(member, row_ids[None, :], row_count), axis=1)
    slots = jnp.arange(pair_rows, dtype=jnp.int32)
    gather_rows = jnp.where(
        slots[None, :] < counts[:, None], starts[:, None] + slots[None, :], row_count
    )
    row_start = jnp.sum(jnp.where(member, starts[:, None], 0), axis=0)
    back_rows = owner_block * pair_rows + (row_ids - row_start)
    return (gather_rows.reshape(-1), back_rows)


def owner_attention(query_in, key_in, value_in, cache_keys, cache_values, lengths, priors, table):
    sources, pair_rows, qcols = query_in.shape
    kcols = key_in.shape[-1]
    kv_heads = kcols // HD
    group = qcols // kcols
    pool_pages = cache_keys.shape[0]
    slots = jnp.arange(pair_rows, dtype=jnp.int32)
    positions = priors[:, None] + slots[None, :]
    live = slots[None, :] < lengths[:, None]
    query_rot = rotary(query_in.reshape(sources, pair_rows, qcols // HD, HD), positions).astype(
        jnp.bfloat16
    )
    key_rot = rotary(key_in.reshape(sources, pair_rows, kv_heads, HD), positions).astype(
        jnp.bfloat16
    )
    key_rot = key_rot.reshape(sources, pair_rows, kcols)
    pages = table.reshape(sources, MAXP)
    page_index = jnp.minimum(positions // PAGE, MAXP - 1)
    target = jnp.take_along_axis(pages, page_index, axis=1)
    target = jnp.where(live, target, pool_pages).reshape(-1)
    offset = (positions % PAGE).reshape(-1)
    keys_out = cache_keys.at[target, offset].set(key_rot.reshape(-1, kcols), mode="drop")
    values_out = cache_values.at[target, offset].set(value_in.reshape(-1, kcols), mode="drop")
    key_block = jnp.take(keys_out, pages.reshape(-1), axis=0).reshape(
        sources, CONTEXT, kv_heads, HD
    )
    value_block = jnp.take(values_out, pages.reshape(-1), axis=0).reshape(
        sources, CONTEXT, kv_heads, HD
    )
    grouped = query_rot.reshape(sources, pair_rows, kv_heads, group, HD)
    scores = (
        jnp.einsum("stkgd,sjkd->skgtj", grouped, key_block, preferred_element_type=jnp.float32)
        * SCORE_MULT
    )
    allowed = (
        jnp.arange(CONTEXT, dtype=jnp.int32)[None, None, None, None, :]
        <= positions[:, None, None, :, None]
    )
    scores = jnp.where(allowed, scores, -jnp.inf)
    top = jnp.max(scores, axis=-1, keepdims=True)
    weights = jnp.exp(scores - top)
    probs = (weights / jnp.sum(weights, axis=-1, keepdims=True)).astype(jnp.bfloat16)
    mixed = jnp.einsum("skgtj,sjkd->stkgd", probs, value_block, preferred_element_type=jnp.float32)
    return (mixed.astype(jnp.bfloat16).reshape(sources, pair_rows, qcols), keys_out, values_out)


def body(
    hidden_in,
    attn_gain,
    mlp_gain,
    w_query,
    w_key,
    w_value,
    w_out,
    w_gate,
    w_up,
    w_down,
    cache_k,
    cache_v,
    owner_of_row,
    new_len,
    prior_len,
    page_table,
):
    peers = lax.axis_size("req")
    groups = lax.axis_size("grp")
    row_count = hidden_in.shape[0]
    pair_rows = 2 * row_count // peers
    quarter = row_count // groups
    group_index = lax.axis_index("grp")
    normed = normalize(hidden_in.astype(jnp.float32), attn_gain).astype(jnp.bfloat16)
    query_rows = jnp.dot(normed, w_query, preferred_element_type=jnp.float32).astype(jnp.bfloat16)
    key_rows = jnp.dot(normed, w_key, preferred_element_type=jnp.float32).astype(jnp.bfloat16)
    value_rows = jnp.dot(normed, w_value, preferred_element_type=jnp.float32).astype(jnp.bfloat16)
    gather_rows, back_rows = source_layout(owner_of_row, peers, pair_rows)
    send_query = jnp.take(query_rows, gather_rows, axis=0, mode="fill", fill_value=0).reshape(
        peers, pair_rows, -1
    )
    send_key = jnp.take(key_rows, gather_rows, axis=0, mode="fill", fill_value=0).reshape(
        peers, pair_rows, -1
    )
    send_value = jnp.take(value_rows, gather_rows, axis=0, mode="fill", fill_value=0).reshape(
        peers, pair_rows, -1
    )
    recv_query, recv_key, recv_value = (
        lax.all_to_all(send_query, "req", split_axis=0, concat_axis=0, tiled=True),
        lax.all_to_all(send_key, "req", split_axis=0, concat_axis=0, tiled=True),
        lax.all_to_all(send_value, "req", split_axis=0, concat_axis=0, tiled=True),
    )
    mixed, keys_out, values_out = owner_attention(
        recv_query, recv_key, recv_value, cache_k, cache_v, new_len[0], prior_len[0], page_table[0]
    )
    returned = lax.all_to_all(mixed, "req", split_axis=0, concat_axis=0, tiled=True)
    attn_rows = jnp.take(returned.reshape(peers * pair_rows, -1), back_rows, axis=0)
    projected = jnp.dot(attn_rows, w_out, preferred_element_type=jnp.float32)
    total = lax.psum(projected.astype(jnp.bfloat16), "grp").astype(jnp.float32)
    attn_part = lax.dynamic_slice_in_dim(total, group_index * quarter, quarter, 0)
    own_rows = lax.dynamic_slice_in_dim(hidden_in, group_index * quarter, quarter, 0).astype(
        jnp.float32
    )
    residual = own_rows + RESIDUAL_MULT * attn_part
    mlp_in = normalize(residual, mlp_gain).astype(jnp.bfloat16)
    piece = lax.all_gather(mlp_in, "req", axis=0, tiled=True)
    gate = jnp.dot(piece, w_gate, preferred_element_type=jnp.float32)
    upper = jnp.dot(piece, w_up, preferred_element_type=jnp.float32)
    hidden = (jax.nn.silu(gate) * upper).astype(jnp.bfloat16)
    down = lax.psum_scatter(
        jnp.dot(hidden, w_down, preferred_element_type=jnp.float32).astype(jnp.bfloat16),
        "req",
        scatter_dimension=0,
        tiled=True,
    ).astype(jnp.float32)
    layer_out = (residual + RESIDUAL_MULT * down).astype(jnp.bfloat16)
    return (layer_out, keys_out, values_out)


def solution(mesh):
    in_specs = (
        P("req", None),
        P(),
        P(),
        P(None, "grp"),
        P(None, "grp"),
        P(None, "grp"),
        P("grp", None),
        P(None, "req"),
        P(None, "req"),
        P("req", None),
        P("req", None, "grp"),
        P("req", None, "grp"),
        P("req"),
        P("req", None),
        P("req", None),
        P("req", None),
    )
    out_specs = (P(("req", "grp"), None), P("req", None, "grp"), P("req", None, "grp"))
    return jax.shard_map(body, mesh=mesh, in_specs=in_specs, out_specs=out_specs, check_vma=False)
```

profile of v0, /device:TPU:0, one launch (start us, length us, event | category | flops | bytes accessed | tf_op | source)
XLA Modules:
  0.0 475.2 jit_solution(9839665422419617770)
XLA Ops:
  7.2 3.4 copy.67
  18.9 3.2 gather_fusion.5
  22.1 3.2 gather_fusion.3
  26.3 8.4 %all-to-all-start.1 = ((bf16[32,32,128]{2,1,0:T(8,128)(2,1)}), bf16[32,32,128]{2,1,0:T(8,128)(2,1)S(1)}, u32[]{:S(2)}, u32[]{:S(2)}) async-start(bf16[32,32,128]{2,1,0:T(8,128)(2,1)} %bitcast.10), calls=%async_computation.1 | async-start | bytes 524288 | tf_op jit(solution)/shard_map/all_to_all | solution.py:137
  37.1 7.1 %gather_fusion.2 = s32[1024]{0:T(1024)S(1)} fusion(s32[32,16]{1,0:T(8,128)S(1)} %reshape_squeeze.3, s32[1024]{0:T(1024)S(1)} %reshape.573), kind=kCustom, calls=%fused_computation.6 | custom fusion | bytes 16384 | tf_op jit(solution)/shard_map/jit(take_along_axis)/gather | solution.py:69
  44.4 3.5 convolution_convert_fusion.2
  48.0 5.1 %gather_fusion = bf16[1024,512]{1,0:T(8,128)(2,1)} fusion(bf16[512,512]{1,0:T(8,128)(2,1)S(1)} %convolution_convert_fusion.2, s32[1024]{0:T(1024)S(1)} %broadcast_clamp_fusion), kind=kCustom, calls=%fused_computation.4 | custom fusion | bytes 2101248 | tf_op jit(solution)/shard_map/jit(_take)/gather | solution.py:126
  56.4 7.5 %all-to-all-start = ((bf16[32,32,128]{2,1,0:T(8,128)(2,1)}), bf16[32,32,128]{2,1,0:T(8,128)(2,1)}, u32[]{:S(2)}, u32[]{:S(2)}) async-start(bf16[32,32,128]{2,1,0:T(8,128)(2,1)} %bitcast.5), calls=%async_computation | async-start | bytes 524288 | tf_op jit(solution)/shard_map/all_to_all | solution.py:138
  63.9 2.9 multiply_cosine_fusion
  67.1 5.7 %all-to-all-done = bf16[32,32,128]{2,1,0:T(8,128)(2,1)} async-done(((bf16[32,32,128]{2,1,0:T(8,128)(2,1)}), bf16[32,32,128]{2,1,0:T(8,128)(2,1)}, u32[]{:S(2)}, u32[]{:S(2)}) %all-to-all-start) | async-done | bytes 262176 | tf_op jit(solution)/shard_map/all_to_all | solution.py:138
  72.9 5.1 %all-to-all-start.2 = ((bf16[32,32,512]{2,1,0:T(8,128)(2,1)}), bf16[32,32,512]{2,1,0:T(8,128)(2,1)}, u32[]{:S(2)}, u32[]{:S(2)}) async-start(bf16[32,32,512]{2,1,0:T(8,128)(2,1)} %broadcast_select_fusion.2), calls=%async_computation.2 | async-start | bytes 2097152 | tf_op jit(solution)/shard_map/all_to_all | solution.py:136
  81.6 6.5 %scatter_fusion.1 = bf16[8192,128]{1,0:T(8,128)(2,1)} fusion(bf16[8192,128]{1,0:T(8,128)(2,1)} %bitcast.52, s32[1024]{0:T(1024)S(1)} %broadcast_select_fusion.5, bf16[1024,128]{1,0:T(8,128)(2,1)S(1)} %reshape.587), kind=kCustom, calls=%fused_computation.8 | custom fusion | bytes 790528
  88.0 4.0 gather_fusion.6
  92.0 6.9 %scatter_fusion = bf16[8192,128]{1,0:T(8,128)(2,1)} fusion(bf16[8192,128]{1,0:T(8,128)(2,1)} %bitcast.49, s32[1024]{0:T(1024)S(1)} %broadcast_select_fusion.5, bf16[1024,128]{1,0:T(8,128)(2,1)} %bitcast.6), kind=kCustom, calls=%fused_computation.7 | custom fusion | bytes 790528
  98.9 4.0 gather_fusion.4
  102.9 4.6 broadcast_select_fusion.1
  107.5 8.2 %reshape.510 = bf16[32,256,2,64]{3,2,1,0:T(2,128)(2,1)} reshape(bf16[512,16,128]{2,1,0:T(8,128)(2,1)} %get-tuple-element.22) | data formatting | bytes 4194304 | tf_op jit(solution)/shard_map/reshape | solution.py:77
  115.7 8.3 %reshape.513 = bf16[32,256,2,64]{3,2,1,0:T(2,128)(2,1)} reshape(bf16[512,16,128]{2,1,0:T(8,128)(2,1)} %get-tuple-element.23) | data formatting | bytes 4194304 | tf_op jit(solution)/shard_map/reshape | solution.py:74
  124.0 3.9 reshape.514
  127.9 4.0 fusion.7
  135.8 4.9 %fusion.49 = (f32[32,2,4,32]{3,2,1,0:T(4,128)S(1)}, f32[32,2,4,32,256]{4,3,2,1,0:T(8,128)}) fusion(f32[32,2,256,32,4]{2,3,4,1,0:T(8,128)S(1)} %fusion.10, pred[32,32,256]{2,1,0:T(8,128)(4,1)S(1)} %copy-done.6), kind=kOutput, calls=%fused_computation.132 | output fusion | flops 12583167 | bytes 17072128 | tf_op jit(solution)/shard_map/sub | solution.py:91
  140.7 4.5 convert_bitcast_fusion
  147.7 4.7 reshape.515
  152.4 7.5 %all-to-all-start.3 = ((bf16[32,32,512]{2,1,0:T(8,128)(2,1)}), bf16[32,32,512]{2,1,0:T(8,128)(2,1)S(1)}, u32[]{:S(2)}, u32[]{:S(2)}) async-start(bf16[32,32,512]{2,1,0:T(8,128)(2,1)} %reshape.515), calls=%async_computation.3 | async-start | bytes 2097152 | tf_op jit(solution)/shard_map/all_to_all | solution.py:143
  159.9 16.7 %all-to-all-done.3 = bf16[32,32,512]{2,1,0:T(8,128)(2,1)S(1)} async-done(((bf16[32,32,512]{2,1,0:T(8,128)(2,1)}), bf16[32,32,512]{2,1,0:T(8,128)(2,1)S(1)}, u32[]{:S(2)}, u32[]{:S(2)}) %all-to-all-start.3) | async-done | bytes 1048608 | tf_op jit(solution)/shard_map/all_to_all | solution.py:143
  176.7 2.6 gather_fusion.1
  179.3 3.7 convolution_convert_fusion.1
  183.1 56.8 %all-reduce.2.cloned.1.call-done = bf16[512,2048]{1,0:T(8,128)(2,1)} async-done(((bf16[512,2048]{1,0:T(8,128)(2,1)}), bf16[512,2048]{1,0:T(8,128)(2,1)}) %all-reduce.2.cloned.1.call-update) | async-done | bytes 2097168 | tf_op jit(solution)/shard_map/psum | solution.py:146
  243.7 72.5 %all-gather.2.cloned.1.call-done = bf16[4096,2048]{1,0:T(8,128)(2,1)} async-done(((bf16[128,2048]{1,0:T(8,128)(2,1)}), bf16[4096,2048]{1,0:T(8,128)(2,1)}) %all-gather.2.cloned.1.call-update) | async-done | bytes 16777232 | tf_op jit(solution)/shard_map/all_gather | solution.py:153
  316.2 10.2 %fusion.50 = f32[4096,256]{1,0:T(8,128)} fusion(bf16[4096,2048]{1,0:T(8,128)(2,1)} %all-gather.2.cloned.1.call-done, bf16[2048,256]{1,0:T(8,128)(2,1)S(1)} %copy-done.14), kind=kOutput, calls=%fused_computation.133 | convolution fusion | flops 4294967296 | bytes 22020096 | tf_op jit(solution)/shard_map/dot_general | solution.py:154
  326.4 24.7 %convolution_convert_fusion = bf16[4096,2048]{1,0:T(8,128)(2,1)} fusion(bf16[256,2048]{1,0:T(8,128)(2,1)} %param.29, bf16[4096,2048]{1,0:T(8,128)(2,1)} %all-gather.2.cloned.1.call-done, bf16[2048,256]{1,0:T(8,128)(2,1)} %param.28, f32[4096,256]{1,0:T(8,128)} %fusion.50), kind=kOutput, calls=%fused_computation.10 | convolution fusion | flops 8604614656 | bytes 39845888 | tf_op jit(solution)/shard_map/dot_general | solution.py:158
  351.2 114.9 %reduce-scatter.2.cloned.1.call-done = bf16[128,2048]{1,0:T(8,128)(2,1)} async-done(((bf16[4096,2048]{1,0:T(8,128)(2,1)}), bf16[128,2048]{1,0:T(8,128)(2,1)}) %reduce-scatter.2.cloned.1.call-update) | async-done | bytes 524304 | tf_op jit(solution)/shard_map/reduce_scatter | solution.py:157
  (100 shorter events, 31.5 us)
Async XLA Ops:
  7.2 172.1 %copy-start = (bf16[512,2048]{1,0:T(8,128)(2,1)S(1)}, bf16[512,2048]{1,0:T(8,128)(2,1)}, u32[]{:S(2)}) copy-start(bf16[512,2048]{1,0:T(8,128)(2,1)} %param.26) | copy-start | bytes 6291460
  7.2 3.4 copy-start.5
  7.2 4.8 %copy-start.8 = (s32[512]{0:T(512)S(1)}, s32[512]{0:T(512)}, u32[]{:S(2)}) copy-start(s32[512]{0:T(512)} %param.32) | copy-start | bytes 6148
  10.6 4.0 copy-start.15
  10.6 4.0 copy-start.16
  12.3 4.6 copy-start.2
  18.8 15.9 %copy-start.7 = (s32[1,512]{1,0:T(1,128)S(1)}, s32[1,512]{1,0:T(1,128)}, u32[]{:S(2)}) copy-start(s32[1,512]{1,0:T(1,128)} %param.35) | copy-start | bytes 6148
  18.8 16.0 %copy-start.10 = (s32[1,32]{1,0:T(1,128)S(1)}, s32[1,32]{1,0:T(1,128)}, u32[]{:S(2)}) copy-start(s32[1,32]{1,0:T(1,128)} %param.34) | copy-start | bytes 388
  18.8 17.6 %copy-start.11 = (s32[1,32]{1,0:T(1,128)S(1)}, s32[1,32]{1,0:T(1,128)}, u32[]{:S(2)}) copy-start(s32[1,32]{1,0:T(1,128)} %param.33) | copy-start | bytes 388
  26.3 30.1 %all-to-all-start.1 = ((bf16[32,32,128]{2,1,0:T(8,128)(2,1)}), bf16[32,32,128]{2,1,0:T(8,128)(2,1)S(1)}, u32[]{:S(2)}, u32[]{:S(2)}) async-start(bf16[32,32,128]{2,1,0:T(8,128)(2,1)} %bitcast.10), calls=%async_computation.1 | async-start | bytes 524288 | tf_op jit(solution)/shard_map/all_to_all | solution.py:137
  37.1 7.2 %copy-start.13 = (s32[2]{0:T(128)S(1)}, s32[2]{0:T(128)}, u32[]{:S(2)}) copy-start(s32[2]{0:T(128)} %constant.139) | copy-start | bytes 28
  37.1 7.3 %copy-start.12 = (s32[2]{0:T(128)S(1)}, s32[2]{0:T(128)}, u32[]{:S(2)}) copy-start(s32[2]{0:T(128)} %constant.136) | copy-start | bytes 28
  56.4 16.4 %all-to-all-start = ((bf16[32,32,128]{2,1,0:T(8,128)(2,1)}), bf16[32,32,128]{2,1,0:T(8,128)(2,1)}, u32[]{:S(2)}, u32[]{:S(2)}) async-start(bf16[32,32,128]{2,1,0:T(8,128)(2,1)} %bitcast.5), calls=%async_computation | async-start | bytes 524288 | tf_op jit(solution)/shard_map/all_to_all | solution.py:138
  72.9 51.2 %all-to-all-start.2 = ((bf16[32,32,512]{2,1,0:T(8,128)(2,1)}), bf16[32,32,512]{2,1,0:T(8,128)(2,1)}, u32[]{:S(2)}, u32[]{:S(2)}) async-start(bf16[32,32,512]{2,1,0:T(8,128)(2,1)} %broadcast_select_fusion.2), calls=%async_computation.2 | async-start | bytes 2097152 | tf_op jit(solution)/shard_map/all_to_all | solution.py:136
  115.7 12.2 %copy-start.3 = (f32[32,32,32]{2,1,0:T(8,128)S(1)}, f32[32,32,32]{2,1,0:T(8,128)}, u32[]{:S(2)}) copy-start(f32[32,32,32]{2,1,0:T(8,128)} %get-tuple-element.16) | copy-start | bytes 393220
  131.9 2.2 copy-start.1
  134.1 1.7 copy-start.6
  135.8 4.9 %copy-start.4 = (bf16[32,256,2,64]{3,2,1,0:T(2,128)(2,1)S(1)}, bf16[32,256,2,64]{3,2,1,0:T(2,128)(2,1)}, u32[]{:S(2)}) copy-start(bf16[32,256,2,64]{3,2,1,0:T(2,128)(2,1)} %reshape.510) | copy-start | bytes 6291460
  152.4 24.3 %all-to-all-start.3 = ((bf16[32,32,512]{2,1,0:T(8,128)(2,1)}), bf16[32,32,512]{2,1,0:T(8,128)(2,1)S(1)}, u32[]{:S(2)}, u32[]{:S(2)}) async-start(bf16[32,32,512]{2,1,0:T(8,128)(2,1)} %reshape.515), calls=%async_computation.3 | async-start | bytes 2097152 | tf_op jit(solution)/shard_map/all_to_all | solution.py:143
  159.8 80.0 %all-reduce.2.cloned.1.call-start = ((), (), s32[]{:S(2)}) async-start(), calls=%async_computation.5 | async-start | bytes 4194304 | tf_op jit(solution)/shard_map/psum | solution.py:146
  179.3 62.1 %copy-start.9 = (f32[2048]{0:T(1024)S(1)}, f32[2048]{0:T(1024)}, u32[]{:S(2)}) copy-start(f32[2048]{0:T(1024)} %param.22) | copy-start | bytes 24580
  183.0 133.2 %copy-start.14 = (bf16[2048,256]{1,0:T(8,128)(2,1)S(1)}, bf16[2048,256]{1,0:T(8,128)(2,1)}, u32[]{:S(2)}) copy-start(bf16[2048,256]{1,0:T(8,128)(2,1)} %param.27) | copy-start | bytes 3145732
  183.0 133.2 %all-gather.2.cloned.1.call-start = ((), (), s32[]{:S(2)}) async-start(), calls=%async_computation.6 | async-start | bytes 17301504 | tf_op jit(solution)/shard_map/all_gather | solution.py:153
  243.6 222.4 %reduce-scatter.2.cloned.1.call-start = ((), (), s32[]{:S(2)}) async-start(), calls=%async_computation.7 | async-start | bytes 17301504 | tf_op jit(solution)/shard_map/reduce_scatter | solution.py:157
Sparse Core Ops, SparseCore 0:
  183.1 56.6 all-reduce.1
  243.8 72.4 all-gather.1
  351.3 114.7 reduce-scatter.1
where the time goes:
time: 482 us; the launch traced here: 475 us
  waiting for transfers between devices  267 us (55%)
  local copies, waits for them, and re-layouts  80.5 us (17%)
  matrix products  52.5 us (11%)
  other arithmetic  32.4 us (7%)
  starting transfers between devices  28.7 us (6%)
  between operations  14.4 us (3%)
    reduce_scatter x1, waiting for transfers between devices, body(): lax.psum_scatter(jnp.dot(hidden, w_down, preferred_element_type=jnp.float...  115 us
    all_gather x1, waiting for transfers between devices, body(): piece = lax.all_gather(mlp_in, 'req', axis=0, tiled=True)  72.5 us
    psum x1, waiting for transfers between devices, body(): total = lax.psum(projected.astype(jnp.bfloat16), 'grp').astype(jnp.float32)  56.8 us
    dot_general x1, matrix products, body(): jnp.dot(hidden, w_down, preferred_element_type=jnp.float32)  24.7 us
    unnamed x39, local copies, waits for them, and re-layouts  19.9 us
    all_to_all x1, waiting for transfers between devices, body(): lax.all_to_all(mixed, 'req', split_axis=0, concat_axis=0, tiled=True)  16.7 us
    dot_general x1, matrix products, body(): gate = jnp.dot(piece, w_gate, preferred_element_type=jnp.float32)  10.2 us
  transfers between devices with their start and end apart: 7, of which 5 were waited for; matrix products, arithmetic and copies ran while one was open for 15% of the time, Pallas kernels for 0%

commit v1 on v0

--- a/solution.py
+++ b/solution.py
@@ -150,7 +150,8 @@
     )
     residual = own_rows + RESIDUAL_MULT * attn_part
     mlp_in = normalize(residual, mlp_gain).astype(jnp.bfloat16)
-    piece = lax.all_gather(mlp_in, "req", axis=0, tiled=True)
+    outgoing = jnp.stack([mlp_in] * lax.axis_size("req"))
+    piece = jnp.concatenate(lax.all_to_all(outgoing, "req", 0, 0), axis=0)
     gate = jnp.dot(piece, w_gate, preferred_element_type=jnp.float32)
     upper = jnp.dot(piece, w_up, preferred_element_type=jnp.float32)
     hidden = (jax.nn.silu(gate) * upper).astype(jnp.bfloat16)

time: 482 us -> 603 us (1.25)
  blocking collectives: 0 us -> 193 us
  waiting for transfers between devices: 267 us -> 191 us
  local copies, waits for them, and re-layouts: 80.5 us -> 88.5 us
    all_to_all x0 -> x1, blocking collectives: none -> 193 us  [body(): piece = jnp.concatenate(lax.all_to_all(outgoing, 'req', 0, 0), axis=0)]
    all_gather x1 -> x0, waiting for transfers between devices: 72.5 us -> none  [body(): piece = lax.all_gather(mlp_in, 'req', axis=0, tiled=True)]
    unnamed x39 -> x47, local copies, waits for them, and re-layouts: 19.9 us -> 25.8 us
  transfers between devices with their start and end apart: 7 -> 6, of which waited for: 5 -> 4; matrix products, arithmetic and copies ran while one was open for 15% -> 12% of each run, Pallas kernels for 0% -> 0%
where the time goes in v1:
time: 603 us; the launch traced here: 596 us
  blocking collectives  193 us (32%)
  waiting for transfers between devices  191 us (32%)
  local copies, waits for them, and re-layouts  88.5 us (15%)
  matrix products  48.1 us (8%)
  other arithmetic  31.7 us (5%)
  starting transfers between devices  28.6 us (5%)
  between operations  14.9 us (2%)
    all_to_all x1, blocking collectives, body(): piece = jnp.concatenate(lax.all_to_all(outgoing, 'req', 0, 0), axis=0)  193 us
    reduce_scatter x1, waiting for transfers between devices, body(): lax.psum_scatter(jnp.dot(hidden, w_down, preferred_element_type=jnp.float...  112 us
    psum x1, waiting for transfers between devices, body(): total = lax.psum(projected.astype(jnp.bfloat16), 'grp').astype(jnp.float32)  56.8 us
    unnamed x47, local copies, waits for them, and re-layouts  25.8 us
    dot_general x1, matrix products, body(): jnp.dot(hidden, w_down, preferred_element_type=jnp.float32)  24.2 us
    all_to_all x1, waiting for transfers between devices, body(): lax.all_to_all(mixed, 'req', split_axis=0, concat_axis=0, tiled=True)  16.7 us
  transfers between devices with their start and end apart: 6, of which 4 were waited for; matrix products, arithmetic and copies ran while one was open for 12% of the time, Pallas kernels for 0%

profile of v1, /device:TPU:0, one launch (start us, length us, event | category | flops | bytes accessed | tf_op | source)
XLA Modules:
  0.0 595.8 jit_solution(4514401828490578951)
XLA Ops:
  7.2 3.4 copy.67
  18.9 3.2 gather_fusion.5
  22.1 3.2 gather_fusion.3
  26.3 8.4 %all-to-all-start.1 = ((bf16[32,32,128]{2,1,0:T(8,128)(2,1)}), bf16[32,32,128]{2,1,0:T(8,128)(2,1)S(1)}, u32[]{:S(2)}, u32[]{:S(2)}) async-start(bf16[32,32,128]{2,1,0:T(8,128)(2,1)} %bitcast.10), calls=%async_computation.1 | async-start | bytes 524288 | tf_op jit(solution)/shard_map/all_to_all | solution.py:137
  37.3 7.1 %gather_fusion.2 = s32[1024]{0:T(1024)S(1)} fusion(s32[32,16]{1,0:T(8,128)S(1)} %reshape_squeeze.3, s32[1024]{0:T(1024)S(1)} %reshape.579), kind=kCustom, calls=%fused_computation.6 | custom fusion | bytes 16384 | tf_op jit(solution)/shard_map/jit(take_along_axis)/gather | solution.py:69
  44.6 3.5 convolution_convert_fusion.2
  48.2 5.1 gather_fusion
  56.6 7.5 %all-to-all-start = ((bf16[32,32,128]{2,1,0:T(8,128)(2,1)}), bf16[32,32,128]{2,1,0:T(8,128)(2,1)}, u32[]{:S(2)}, u32[]{:S(2)}) async-start(bf16[32,32,128]{2,1,0:T(8,128)(2,1)} %bitcast.5), calls=%async_computation | async-start | bytes 524288 | tf_op jit(solution)/shard_map/all_to_all | solution.py:138
  64.2 2.9 multiply_cosine_fusion
  67.4 5.7 all-to-all-done
  73.1 5.1 all-to-all-start.2
  81.8 6.5 %scatter_fusion.1 = bf16[8192,128]{1,0:T(8,128)(2,1)} fusion(bf16[8192,128]{1,0:T(8,128)(2,1)} %bitcast.53, s32[1024]{0:T(1024)S(1)} %broadcast_select_fusion.5, bf16[1024,128]{1,0:T(8,128)(2,1)S(1)} %reshape.593), kind=kCustom, calls=%fused_computation.8 | custom fusion | bytes 790528
  88.3 4.0 gather_fusion.6
  92.2 6.9 %scatter_fusion = bf16[8192,128]{1,0:T(8,128)(2,1)} fusion(bf16[8192,128]{1,0:T(8,128)(2,1)} %bitcast.50, s32[1024]{0:T(1024)S(1)} %broadcast_select_fusion.5, bf16[1024,128]{1,0:T(8,128)(2,1)} %bitcast.6), kind=kCustom, calls=%fused_computation.7 | custom fusion | bytes 790528
  99.2 4.0 gather_fusion.4
  103.2 4.6 broadcast_select_fusion.1
  107.7 8.2 %reshape.515 = bf16[32,256,2,64]{3,2,1,0:T(2,128)(2,1)} reshape(bf16[512,16,128]{2,1,0:T(8,128)(2,1)} %get-tuple-element.22) | data formatting | bytes 4194304 | tf_op jit(solution)/shard_map/reshape | solution.py:77
  116.0 8.3 %reshape.518 = bf16[32,256,2,64]{3,2,1,0:T(2,128)(2,1)} reshape(bf16[512,16,128]{2,1,0:T(8,128)(2,1)} %get-tuple-element.23) | data formatting | bytes 4194304 | tf_op jit(solution)/shard_map/reshape | solution.py:74
  124.2 3.9 reshape.519
  128.1 4.0 fusion.7
  136.0 4.9 fusion.49
  140.9 4.5 convert_bitcast_fusion
  147.9 4.7 reshape.520
  152.6 7.5 %all-to-all-start.3 = ((bf16[32,32,512]{2,1,0:T(8,128)(2,1)}), bf16[32,32,512]{2,1,0:T(8,128)(2,1)S(1)}, u32[]{:S(2)}, u32[]{:S(2)}) async-start(bf16[32,32,512]{2,1,0:T(8,128)(2,1)} %reshape.520), calls=%async_computation.3 | async-start | bytes 2097152 | tf_op jit(solution)/shard_map/all_to_all | solution.py:143
  160.2 16.7 %all-to-all-done.3 = bf16[32,32,512]{2,1,0:T(8,128)(2,1)S(1)} async-done(((bf16[32,32,512]{2,1,0:T(8,128)(2,1)}), bf16[32,32,512]{2,1,0:T(8,128)(2,1)S(1)}, u32[]{:S(2)}, u32[]{:S(2)}) %all-to-all-start.3) | async-done | bytes 1048608 | tf_op jit(solution)/shard_map/all_to_all | solution.py:143
  179.5 3.7 convolution_convert_fusion.1
  183.3 56.8 %all-reduce.2.cloned.1.call-done = bf16[512,2048]{1,0:T(8,128)(2,1)} async-done(((bf16[512,2048]{1,0:T(8,128)(2,1)}), bf16[512,2048]{1,0:T(8,128)(2,1)}) %all-reduce.2.cloned.1.call-update) | async-done | bytes 2097168 | tf_op jit(solution)/shard_map/psum | solution.py:146
  245.2 192.5 %all_to_all.25 = bf16[32,128,2048]{2,1,0:T(8,128)(2,1)S(1)} all-to-all(bf16[32,128,2048]{2,1,0:T(8,128)(2,1)S(1)} %stack.2), channel_id=1, replica_groups=mesh['req'=32,'grp'=4] {'req'}, dimensions={0} | all-to-all | bytes 33554432 | tf_op jit(solution)/shard_map/all_to_all | solution.py:154
  437.7 5.7 copy-done.2
  443.5 6.3 %fusion.50 = f32[4096,256]{1,0:T(8,128)} fusion(bf16[4096,2048]{1,0:T(8,128)(2,1)S(1)} %bitcast.56, bf16[2048,256]{1,0:T(8,128)(2,1)S(1)} %copy-done.16), kind=kOutput, calls=%fused_computation.133 | convolution fusion | flops 4294967296 | bytes 22020096 | tf_op jit(solution)/shard_map/dot_general | solution.py:155
  449.8 24.2 %convolution_convert_fusion = bf16[4096,2048]{1,0:T(8,128)(2,1)} fusion(bf16[256,2048]{1,0:T(8,128)(2,1)S(1)} %copy-done.17, bf16[4096,2048]{1,0:T(8,128)(2,1)} %bitcast.57, bf16[2048,256]{1,0:T(8,128)(2,1)S(1)} %copy-done.18, f32[4096,256]{1,0:T(8,128)} %fusion.50), kind=kOutput, calls=%fused_computation.10 | convolution fusion | flops 8604614656 | bytes 39845888 | tf_op jit(solution)/shard_map/dot_general | solution.py:159
  474.1 112.1 %reduce-scatter.2.cloned.1.call-done = bf16[128,2048]{1,0:T(8,128)(2,1)} async-done(((bf16[4096,2048]{1,0:T(8,128)(2,1)}), bf16[128,2048]{1,0:T(8,128)(2,1)}) %reduce-scatter.2.cloned.1.call-update) | async-done | bytes 524304 | tf_op jit(solution)/shard_map/reduce_scatter | solution.py:158
  (107 shorter events, 35.6 us)
Async XLA Ops:
  7.2 172.3 %copy-start = (bf16[512,2048]{1,0:T(8,128)(2,1)S(1)}, bf16[512,2048]{1,0:T(8,128)(2,1)}, u32[]{:S(2)}) copy-start(bf16[512,2048]{1,0:T(8,128)(2,1)} %param.26) | copy-start | bytes 6291460
  7.2 3.4 copy-start.7
  7.2 4.8 copy-start.10
  10.6 4.0 copy-start.19
  10.6 4.0 copy-start.20
  12.3 4.7 copy-start.4
  18.8 15.9 %copy-start.9 = (s32[1,512]{1,0:T(1,128)S(1)}, s32[1,512]{1,0:T(1,128)}, u32[]{:S(2)}) copy-start(s32[1,512]{1,0:T(1,128)} %param.35) | copy-start | bytes 6148
  18.8 16.0 %copy-start.12 = (s32[1,32]{1,0:T(1,128)S(1)}, s32[1,32]{1,0:T(1,128)}, u32[]{:S(2)}) copy-start(s32[1,32]{1,0:T(1,128)} %param.34) | copy-start | bytes 388
  18.9 17.9 %copy-start.13 = (s32[1,32]{1,0:T(1,128)S(1)}, s32[1,32]{1,0:T(1,128)}, u32[]{:S(2)}) copy-start(s32[1,32]{1,0:T(1,128)} %param.33) | copy-start | bytes 388
  26.3 30.3 %all-to-all-start.1 = ((bf16[32,32,128]{2,1,0:T(8,128)(2,1)}), bf16[32,32,128]{2,1,0:T(8,128)(2,1)S(1)}, u32[]{:S(2)}, u32[]{:S(2)}) async-start(bf16[32,32,128]{2,1,0:T(8,128)(2,1)} %bitcast.10), calls=%async_computation.1 | async-start | bytes 524288 | tf_op jit(solution)/shard_map/all_to_all | solution.py:137
  37.3 7.2 %copy-start.15 = (s32[2]{0:T(128)S(1)}, s32[2]{0:T(128)}, u32[]{:S(2)}) copy-start(s32[2]{0:T(128)} %constant.139) | copy-start | bytes 28
  37.3 7.3 %copy-start.14 = (s32[2]{0:T(128)S(1)}, s32[2]{0:T(128)}, u32[]{:S(2)}) copy-start(s32[2]{0:T(128)} %constant.136) | copy-start | bytes 28
  56.6 16.4 %all-to-all-start = ((bf16[32,32,128]{2,1,0:T(8,128)(2,1)}), bf16[32,32,128]{2,1,0:T(8,128)(2,1)}, u32[]{:S(2)}, u32[]{:S(2)}) async-start(bf16[32,32,128]{2,1,0:T(8,128)(2,1)} %bitcast.5), calls=%async_computation | async-start | bytes 524288 | tf_op jit(solution)/shard_map/all_to_all | solution.py:138
  73.1 51.2 %all-to-all-start.2 = ((bf16[32,32,512]{2,1,0:T(8,128)(2,1)}), bf16[32,32,512]{2,1,0:T(8,128)(2,1)}, u32[]{:S(2)}, u32[]{:S(2)}) async-start(bf16[32,32,512]{2,1,0:T(8,128)(2,1)} %broadcast_select_fusion.2), calls=%async_computation.2 | async-start | bytes 2097152 | tf_op jit(solution)/shard_map/all_to_all | solution.py:136
  116.0 12.2 %copy-start.5 = (f32[32,32,32]{2,1,0:T(8,128)S(1)}, f32[32,32,32]{2,1,0:T(8,128)}, u32[]{:S(2)}) copy-start(f32[32,32,32]{2,1,0:T(8,128)} %get-tuple-element.16) | copy-start | bytes 393220
  132.2 2.2 copy-start.3
  134.4 1.7 copy-start.8
  136.0 4.9 copy-start.6
  152.6 24.3 %all-to-all-start.3 = ((bf16[32,32,512]{2,1,0:T(8,128)(2,1)}), bf16[32,32,512]{2,1,0:T(8,128)(2,1)S(1)}, u32[]{:S(2)}, u32[]{:S(2)}) async-start(bf16[32,32,512]{2,1,0:T(8,128)(2,1)} %reshape.520), calls=%async_computation.3 | async-start | bytes 2097152 | tf_op jit(solution)/shard_map/all_to_all | solution.py:143
  160.1 80.1 %all-reduce.2.cloned.1.call-start = ((), (), s32[]{:S(2)}) async-start(), calls=%async_computation.6 | async-start | bytes 4194304 | tf_op jit(solution)/shard_map/psum | solution.py:146
  179.5 62.1 %copy-start.11 = (f32[2048]{0:T(1024)S(1)}, f32[2048]{0:T(1024)}, u32[]{:S(2)}) copy-start(f32[2048]{0:T(1024)} %param.22) | copy-start | bytes 24580
  183.3 402.9 %reduce-scatter.2.cloned.1.call-start = ((), (), s32[]{:S(2)}) async-start(), calls=%async_computation.7 | async-start | bytes 17301504 | tf_op jit(solution)/shard_map/reduce_scatter | solution.py:158
  245.2 198.3 %copy-start.16 = (bf16[2048,256]{1,0:T(8,128)(2,1)S(1)}, bf16[2048,256]{1,0:T(8,128)(2,1)}, u32[]{:S(2)}) copy-start(bf16[2048,256]{1,0:T(8,128)(2,1)} %param.27) | copy-start | bytes 3145732
  437.7 5.7 copy-start.2
  443.5 6.3 %copy-start.17 = (bf16[256,2048]{1,0:T(8,128)(2,1)S(1)}, bf16[256,2048]{1,0:T(8,128)(2,1)}, u32[]{:S(2)}) copy-start(bf16[256,2048]{1,0:T(8,128)(2,1)} %param.29) | copy-start | bytes 3145732
  443.5 6.3 %copy-start.18 = (bf16[2048,256]{1,0:T(8,128)(2,1)S(1)}, bf16[2048,256]{1,0:T(8,128)(2,1)}, u32[]{:S(2)}) copy-start(bf16[2048,256]{1,0:T(8,128)(2,1)} %param.28) | copy-start | bytes 3145732
  474.1 114.5 %copy-start.1 = (bf16[512,2048]{1,0:T(8,128)(2,1)S(1)}, bf16[512,2048]{1,0:T(8,128)(2,1)}, u32[]{:S(2)}) copy-start(bf16[512,2048]{1,0:T(8,128)(2,1)} %param.26) | copy-start | bytes 6291460
Sparse Core Ops, SparseCore 0:
  183.4 56.7 all-reduce.1
  474.2 111.8 reduce-scatter.1
